TPU v7x, 32 devices: a whole 2x2x4 slice. The times are simulated.
32 devices in a mesh: video: 2 (over y), block: 4 (over z), band: 2 (over x), chan: 2 (over core).
Axes of the slice: x: 2, y: 2, z: 4, core: 2. Of those that a mesh axis runs over, the one named last changes fastest.
Arguments:
- latents: bfloat16 [32, 2, 1664], P(('video', 'block'), 'band'), parts along dimension 0, may hold values from -60 to 60
- frame_counts: int32 [8], P('video'), parts along dimension 0, may hold values from 1 to 4, 8 in all
- w_in: bfloat16 [3, 3, 3, 16, 384], replicated, may hold values from -0.3125 to 0.3125
- gain_in: float32 [384], replicated, may hold values from 0.1 to 1.9
- shift_in: float32 [384], replicated, may hold values from -3 to 3
- w_mid: bfloat16 [3, 3, 3, 384, 384], P(None, None, None, None, 'chan'), may hold values from -0.0625 to 0.0625
- gain_out: float32 [384], P('chan'), may hold values from 0.1 to 1.9
- shift_out: float32 [384], P('chan'), may hold values from -3 to 3
Outputs:
- decoded: bfloat16 [32, 2, 104, 384], P(('video', 'block'), 'band', None, 'chan'), parts along dimension 0
There are 2 independent parts, one for each index of `video`. A program takes and returns all parts, laid end to end along the dimension named above; an argument that names none is the same for every part. Nothing has to cross between parts.
Inputs may be any that keep to these rules, and one draw needn't show every extreme that they name: `frame_counts`: entry k is the number of consecutive latent frames that device k of the frame axis holds; the entries sum to 8.
All inputs are finite; a program needn't handle non-finite values.
Results may differ from a plain program's by a relative error of at most 0.013.
Values may be sent and summed in bfloat16 or wider, within the bound.
No kernel may reach another device: no remote copies, remote signals or barrier semaphores. Data moves between devices by JAX's collectives and lax.ppermute only.
A program may use at most 64 MiB of HBM per device.

v0:
```python
import jax
import jax.numpy as jnp
from jax import lax
from jax.sharding import PartitionSpec as P

LAT = 16
C = 384
GROUPS = 32
EPSILON = 1e-06


def with_halo(cells, sides, width):
    for axis, dim in sides:
        count = lax.axis_size(axis)
        ends = count - 1
        head = lax.slice_in_dim(cells, 0, width, axis=dim)
        tail = lax.slice_in_dim(cells, cells.shape[dim] - width, cells.shape[dim], axis=dim)
        cells = jnp.concatenate(
            [
                lax.ppermute(tail, axis, [(i, (i + 1) % count) for i in range(ends)]),
                cells,
                lax.ppermute(head, axis, [((i + 1) % count, i) for i in range(ends)]),
            ],
            axis=dim,
        )
    return cells


def count_for(frame_counts, position):
    places = jnp.arange(frame_counts.shape[0], dtype=jnp.int32)
    return jnp.sum(jnp.where(places == position, frame_counts, 0))


def start_for(frame_counts, position):
    places = jnp.arange(frame_counts.shape[0], dtype=jnp.int32)
    return jnp.sum(jnp.where(places < position, frame_counts, 0))


def rows_beside(values):
    return with_halo(values, (("band", 1),), 1)


def group_silu(values, norm_gain, norm_shift):
    in_frames, band_rows, columns, local_width = values.shape
    group_width = C // GROUPS
    local_groups = local_width // group_width
    grouped = values.reshape(in_frames, band_rows * columns, local_groups, group_width)
    group_total, squares = lax.psum(
        (jnp.sum(grouped, axis=(1, 3)), jnp.sum(grouped * grouped, axis=(1, 3))), "band"
    )
    total = float(lax.axis_size("band") * band_rows * columns * group_width)
    group_mean = group_total / total
    variance = squares / total - group_mean * group_mean
    inverse = lax.rsqrt(variance + EPSILON)
    normed = (grouped - group_mean[:, None, :, None]) * inverse[:, None, :, None]
    normed = normed.reshape(values.shape)
    return jax.nn.silu(normed * norm_gain + norm_shift)


def latent_conv(extended, kernel):
    steps_in, rows_padded, flat_width = extended.shape
    lat_width = kernel.shape[3]
    out_width = kernel.shape[4]
    columns = flat_width // lat_width
    out_frames = steps_in - 2
    band_rows = rows_padded - 2
    latent_grid = extended.reshape(steps_in, rows_padded, columns, lat_width)
    latent_grid = jnp.pad(latent_grid, ((0, 0), (0, 0), (1, 1), (0, 0)))
    patches = []
    for step_t in range(3):
        for step_y in range(3):
            for step_x in range(3):
                patches.append(
                    latent_grid[
                        step_t : step_t + out_frames,
                        step_y : step_y + band_rows,
                        step_x : step_x + columns,
                        :,
                    ]
                )
    stacked = jnp.concatenate(patches, axis=-1).reshape(-1, 27 * lat_width)
    result = jnp.dot(
        stacked, kernel.reshape(27 * lat_width, out_width), preferred_element_type=jnp.float32
    )
    return result.reshape(out_frames, band_rows, columns, out_width)


def weighted_taps(padded, kernel):
    in_frames, rows_padded, cols_padded, in_width = padded.shape
    out_frames = in_frames - 2
    band_rows = rows_padded - 2
    columns = cols_padded - 2
    out_width = kernel.shape[4]
    accumulate = jnp.zeros((out_frames * band_rows * columns, out_width), jnp.float32)
    for step_t in range(3):
        for step_y in range(3):
            patches = [
                padded[
                    step_t : step_t + out_frames,
                    step_y : step_y + band_rows,
                    step_x : step_x + columns,
                    :,
                ]
                for step_x in range(3)
            ]
            stacked = jnp.concatenate(patches, axis=-1).reshape(-1, 3 * in_width)
            accumulate = accumulate + jnp.dot(
                stacked,
                kernel[step_t, step_y].reshape(3 * in_width, out_width),
                preferred_element_type=jnp.float32,
            )
    return accumulate.reshape(out_frames, band_rows, columns, out_width)


def middle_section(act_extended, w_mid, gain_out, shift_out):
    padded = jnp.pad(rows_beside(act_extended), ((0, 0), (0, 0), (1, 1), (0, 0)))
    second_conv = weighted_taps(lax.all_gather(padded, "chan", axis=3, tiled=True), w_mid)
    second_conv = second_conv.astype(jnp.bfloat16)
    return group_silu(second_conv.astype(jnp.float32), gain_out, shift_out).astype(jnp.bfloat16)


def shards(latents, frame_counts, w_in, gain_in, shift_in, w_mid, gain_out, shift_out):
    frames, band_rows, flat_width = latents.shape
    columns = flat_width // LAT
    half_width = w_mid.shape[4]
    position = lax.axis_index("block")
    live_count = count_for(frame_counts, position)
    offset = lax.axis_index("chan") * half_width
    front_kernel = lax.dynamic_slice_in_dim(w_in, offset, half_width, 4)
    front_gain = lax.dynamic_slice_in_dim(gain_in, offset, half_width, 0)
    front_shift = lax.dynamic_slice_in_dim(shift_in, offset, half_width, 0)
    share = frames // 2
    all_slots = lax.all_gather(latents, "block", axis=0, tiled=True)
    run_ends = jnp.cumsum(frame_counts)
    run_starts = run_ends - frame_counts
    first_frame = position * share - 4
    wanted = first_frame + jnp.arange(share + 4, dtype=jnp.int32)
    owners = jnp.sum((wanted[:, None] >= run_ends[None, :]).astype(jnp.int32), axis=1)
    slot_ids = owners * frames + wanted - jnp.take(run_starts, owners)
    slot_ids = jnp.clip(slot_ids, 0, all_slots.shape[0] - 1)
    picked = jnp.take(all_slots, slot_ids, axis=0)
    latent_extended = jnp.where((wanted >= 0)[:, None, None], picked, jnp.zeros_like(picked))
    first_conv = latent_conv(rows_beside(latent_extended), front_kernel).astype(jnp.bfloat16)
    activated = group_silu(first_conv.astype(jnp.float32), front_gain, front_shift).astype(
        jnp.bfloat16
    )
    act_ids = first_frame + 2 + jnp.arange(share + 2, dtype=jnp.int32)
    act_extended = jnp.where(
        (act_ids >= 0)[:, None, None, None], activated, jnp.zeros_like(activated)
    )
    even_norm = middle_section(act_extended, w_mid, gain_out, shift_out)
    my_start = start_for(frame_counts, position)
    slot_places = jnp.arange(frames, dtype=jnp.int32)
    slot_frames = my_start + slot_places
    slot_alive = slot_places < live_count
    initial = jnp.zeros((frames, band_rows, columns, half_width), jnp.bfloat16)
    piece = lax.all_gather(even_norm, "block", axis=0, tiled=True)
    valid = (slot_frames >= 0) & (slot_frames < piece.shape[0]) & slot_alive
    took = jnp.take(piece, jnp.clip(slot_frames, 0, piece.shape[0] - 1), axis=0)
    return jnp.where(valid[:, None, None, None], took, initial)


def solution(mesh):
    return jax.shard_map(
        shards,
        mesh=mesh,
        in_specs=(
            P(("video", "block"), "band", None),
            P("video"),
            P(),
            P(),
            P(),
            P(None, None, None, None, "chan"),
            P("chan"),
            P("chan"),
        ),
        out_specs=P(("video", "block"), "band", None, "chan"),
        check_vma=False,
    )
```

profile of v0, /device:TPU:0, one launch (start us, length us, event | category | flops | bytes accessed | tf_op | source)
XLA Modules:
  0.0 121.1 jit_solution(8071006151488944462)
XLA Ops:
  0.0 0.9 reduce-window.8
  0.9 1.3 %fusion.23 = (s32[]{:T(128)}, s32[]{:T(128)}, s32[4]{0:T(128)S(1)}) fusion(s32[4]{0:T(128)} %param.9, s32[]{:T(128)S(6)} %axis_index.23, s32[4,1]{0,1:T(1,128)S(1)} %reduce-window.8), kind=kLoop, calls=%fused_computation.78 | loop fusion | flops 26 | bytes 60 | tf_op jit(solution)/shard_map/reduce_sum | solution.py:31
  2.3 0.6 gather_fusion
  3.0 0.7 copy.111
  3.7 15.1 %all_gather.9 = bf16[16,1,1664]{2,1,0:T(2,128)(2,1)S(1)} all-gather(bf16[4,1,1664]{2,1,0:T(2,128)(2,1)S(1)} %copy.111), channel_id=1, replica_groups=mesh['video'=2,'block'=4,'band'=2,'chan'=2] {'block'}, dimensions={0}, use_global_device_ids=true | all-gather | bytes 66560 | tf_op jit(solution)/shard_map/all_gather | solution.py:133
  18.9 0.6 gather_fusion.1
  19.5 1.3 %collective-permute-start.1 = (bf16[6,1,1664]{2,0,1:T(8,128)(2,1)S(1)}, bf16[6,1,1664]{2,0,1:T(8,128)(2,1)S(1)}, u32[]{:S(2)}, u32[]{:S(2)}) collective-permute-start(bf16[6,1,1664]{2,0,1:T(8,128)(2,1)S(1)} %fusion.21), channel_id=1, source_target_pairs={{2,0},{3,1},{6,4},{7,5},{10,8},{11,9},{14,12},{15,13},{18,16},{19,... | collective-permute-start | bytes 59912 | tf_op jit(solution)/shard_map/ppermute | solution.py:22
  20.8 4.5 %collective-permute-start = (bf16[6,1,1664]{2,0,1:T(8,128)(2,1)S(1)}, bf16[6,1,1664]{2,0,1:T(8,128)(2,1)S(1)}, u32[]{:S(2)}, u32[]{:S(2)}) collective-permute-start(bf16[6,1,1664]{2,0,1:T(8,128)(2,1)S(1)} %fusion.21), channel_id=1, source_target_pairs={{0,2},{1,3},{4,6},{5,7},{8,10},{9,11},{12,14},{13,15},{16,18},{17,... | collective-permute-start | bytes 59912 | tf_op jit(solution)/shard_map/ppermute | solution.py:20
  25.6 0.8 fusion.36
  26.4 3.6 %fusion.32 = (bf16[1,1,3,384,192]{3,4,2,1,0:T(8,128)(2,1)S(1)}, bf16[1,1,3,384,192]{3,4,2,1,0:T(8,128)(2,1)S(1)}, bf16[1,1,3,384,192]{3,4,2,1,0:T(8,128)(2,1)S(1...) fusion(bf16[3,3,3,384,192]{3,4,2,1,0:T(8,128)(2,1)} %param.13), kind=kLoop, calls=%fused_computation.95 | loop fusion | bytes 7962624 | tf_op jit(solution)/shard_map/slice | solution.py:109
  29.9 0.8 constant_dynamic-slice_fusion
  30.8 1.8 %compare_and_fusion.1 = (pred[4]{0:T(512)(128)(4,1)}, pred[4]{0:T(512)(128)(4,1)}) fusion(s32[]{:T(128)} %get-tuple-element.10, s32[]{:T(128)} %get-tuple-element.9), kind=kLoop, calls=%fused_computation.71 | loop fusion | flops 52 | bytes 16 | tf_op jit(solution)/shard_map/jit(_take)/and | solution.py:159
  32.6 0.6 add_compare_fusion
  33.2 0.7 dynamic_slice.11
  33.8 0.7 dynamic_slice.10
  35.1 1.3 %fusion.35 = (bf16[4,1,104,16]{3,2,0,1:T(8,128)(2,1)}, bf16[4,1,104,16]{3,2,0,1:T(8,128)(2,1)}, bf16[4,1,104,16]{3,2,0,1:T(8,128)(2,1)}, bf16[4,1,104,16]{3,2,0,...) fusion(bf16[6,3,106,16]{3,2,0,1:T(8,128)(2,1)S(1)} %fusion.14), kind=kLoop, calls=%fused_computation.98 | loop fusion | bytes 479232 | tf_op jit(solution)/shard_map/slice | solution.py:74
  36.5 0.6 fusion.37
  37.2 0.8 slice.234
  38.0 0.8 slice.238
  38.8 1.5 %slice.245 = bf16[4,1,104,16]{3,2,0,1:T(8,128)(2,1)} reshape(bf16[4,1,1664]{2,0,1:T(4,128)(2,1)} %get-tuple-element.73) | data formatting | bytes 26624 | tf_op jit(solution)/shard_map/slice | solution.py:74
  40.3 0.8 slice.249
  41.1 1.5 %slice.256 = bf16[4,1,104,16]{3,2,0,1:T(8,128)(2,1)} reshape(bf16[4,1,1664]{2,0,1:T(4,128)(2,1)} %get-tuple-element.72) | data formatting | bytes 26624 | tf_op jit(solution)/shard_map/slice | solution.py:74
  42.6 4.0 %concatenate.44 = bf16[4,1,104,432]{3,2,0,1:T(8,128)(2,1)} concatenate(bf16[4,1,104,16]{3,2,0,1:T(8,128)(2,1)} %get-tuple-element.68, bf16[4,1,104,16]{3,2,0,1:T(8,128)(2,1)S(1)} %slice.227, bf16[4,1,104,16]{3,2,0,1:T(8,128)(2,1)} %get-tuple-element.67, bf16[4,1,104,16]{3,2,0,1:T(8,128)(2,1)} %get-tuple-element.66, bf16[4,1,104,16]{3,2,0,1:T(8,128)(2,1)S(1)} %copy-done.18, ...), dimensions={3} | concatenate | bytes 718848 | tf_op jit(solution)/shard_map/concatenate | solution.py:81
  46.6 2.2 %fusion.30 = (f32[4,192]{1,0:T(4,128)S(1)}, f32[4,192]{1,0:T(4,128)S(1)}, f32[4,104,192]{1,2,0:T(8,128)}) fusion(bf16[432,192,1]{1,0,2:T(8,128)(2,1)} %bitcast.174, bf16[4,1,104,432]{3,2,0,1:T(8,128)(2,1)} %concatenate.44), kind=kOutput, calls=%fused_computation.93 | convolution fusion | flops 69407232 | bytes 850944 | tf_op jit(solution)/shard_map/dot_general | solution.py:82
  49.1 4.9 %all-reduce.3 = (f32[4,16]{1,0:T(4,128)S(1)}, f32[4,16]{1,0:T(4,128)S(1)}) all-reduce(f32[4,16]{1,0:T(4,128)S(1)} %reduce_sum.88, f32[4,16]{1,0:T(4,128)S(1)} %reduce_sum.85), channel_id=1, replica_groups=mesh['video'=2,'block'=4,'band'=2,'chan'=2] {'band'}, use_global_device_ids=true, to_apply=%region_9.10 | all-reduce | flops 128 | bytes 1024 | tf_op jit(solution)/shard_map/psum | solution.py:48
  54.4 1.3 %select_bitcast_fusion = bf16[4,1,104,192]{2,3,0,1:T(8,128)(2,1)S(1)} fusion(f32[192]{0:T(256)S(1)} %copy-done.19, f32[192]{0:T(256)S(1)} %copy-done.20, f32[4,192]{1,0:T(4,128)S(1)} %mul.122, f32[4,104,192]{1,2,0:T(8,128)} %get-tuple-element.83, f32[4,192]{1,0:T(4,128)S(1)} %sub.66, pred[4]{0:T(512)(128)(4,1)S(1)} %copy-done.27), kind=kLoop, calls=%fused_computation.52 | loop fusion | flops 798720 | bytes 486916 | tf_op jit(solution)/shard_map/jit(_where)/select_n | solution.py:148
  55.8 1.3 %collective-permute-start.3 = (bf16[4,1,104,192]{2,3,0,1:T(8,128)(2,1)S(1)}, bf16[4,1,104,192]{2,3,0,1:T(8,128)(2,1)S(1)}, u32[]{:S(2)}, u32[]{:S(2)}) collective-permute-start(bf16[4,1,104,192]{2,3,0,1:T(8,128)(2,1)S(1)} %select_bitcast_fusion), channel_id=1, source_target_pairs={{2,0},{3,1},{6,4},{7,5},{10,8},{11,9},{14,12},{15,13},{18,16},{19,... | collective-permute-start | bytes 479240 | tf_op jit(solution)/shard_map/ppermute | solution.py:22
  57.1 4.6 %collective-permute-start.2 = (bf16[4,1,104,192]{2,3,0,1:T(8,128)(2,1)S(1)}, bf16[4,1,104,192]{2,3,0,1:T(8,128)(2,1)S(1)}, u32[]{:S(2)}, u32[]{:S(2)}) collective-permute-start(bf16[4,1,104,192]{2,3,0,1:T(8,128)(2,1)S(1)} %select_bitcast_fusion), channel_id=1, source_target_pairs={{0,2},{1,3},{4,6},{5,7},{8,10},{9,11},{12,14},{13,15},{16,18},{17,... | collective-permute-start | bytes 479240 | tf_op jit(solution)/shard_map/ppermute | solution.py:20
  61.7 0.6 fusion.27
  62.3 0.4 copy.114
  62.7 0.8 copy.138
  63.8 0.4 copy.116
  64.2 0.8 copy.139
  65.3 0.4 copy.118
  65.7 0.8 copy.140
  66.6 0.4 copy.120
  67.0 0.8 copy.141
  67.8 0.4 copy.122
  68.2 0.8 copy.142
  69.0 0.4 copy.124
  69.4 0.8 copy.143
  70.2 0.4 copy.126
  70.6 0.8 copy.144
  71.4 0.4 copy.128
  71.8 0.8 copy.145
  73.0 0.8 copy.146
  74.2 2.8 %all_gather.10 = bf16[4,3,106,384]{2,3,0,1:T(8,128)(2,1)S(1)} all-gather(bf16[4,3,106,192]{2,3,0,1:T(8,128)(2,1)S(1)} %fusion.12), channel_id=1, replica_groups=mesh['video'=2,'block'=4,'band'=2,'chan'=2] {'chan'}, dimensions={3}, use_global_device_ids=true | all-gather | bytes 1465344 | tf_op jit(solution)/shard_map/all_gather | solution.py:117
  77.4 2.3 %fusion.33 = (bf16[2,1,104,384]{2,3,0,1:T(8,128)(2,1)S(1)}, bf16[2,1,104,384]{2,3,0,1:T(8,128)(2,1)}, bf16[2,1,104,384]{2,3,0,1:T(8,128)(2,1)}, bf16[2,1,104,384...) fusion(bf16[4,3,106,384]{2,3,0,1:T(8,128)(2,1)S(1)} %all_gather.10), kind=kLoop, calls=%fused_computation.96 | loop fusion | bytes 6070272 | tf_op jit(solution)/shard_map/slice | solution.py:98
  79.8 1.0 copy.113
  81.2 0.6 copy-done.15
  82.3 1.1 pad_maximum_fusion.3
  83.7 1.0 pad_maximum_fusion.4
  85.1 1.2 %pad_maximum_fusion.5 = bf16[2,1,104,1152]{2,3,0,1:T(8,128)(2,1)S(1)} fusion(bf16[2,1,104,384]{2,3,0,1:T(8,128)(2,1)} %get-tuple-element.33, bf16[2,1,104,384]{2,3,0,1:T(8,128)(2,1)} %get-tuple-element.34, bf16[2,1,104,384]{2,3,0,1:T(8,128)(2,1)} %get-tuple-element.35), kind=kLoop, calls=%fused_computation.34 | loop fusion | flops 1437696 | bytes 958464 | tf_op jit(solution)/shard_map/concatenate | solution.py:106
  86.6 1.2 %pad_maximum_fusion.6 = bf16[2,1,104,1152]{2,3,0,1:T(8,128)(2,1)S(1)} fusion(bf16[2,1,104,384]{2,3,0,1:T(8,128)(2,1)} %get-tuple-element.30, bf16[2,1,104,384]{2,3,0,1:T(8,128)(2,1)} %get-tuple-element.31, bf16[2,1,104,384]{2,3,0,1:T(8,128)(2,1)} %get-tuple-element.32), kind=kLoop, calls=%fused_computation.35 | loop fusion | flops 1437696 | bytes 958464 | tf_op jit(solution)/shard_map/concatenate | solution.py:106
  87.8 1.1 copy.125
  88.9 1.2 %pad_maximum_fusion.7 = bf16[2,1,104,1152]{2,3,0,1:T(8,128)(2,1)S(1)} fusion(bf16[2,1,104,384]{2,3,0,1:T(8,128)(2,1)} %get-tuple-element.27, bf16[2,1,104,384]{2,3,0,1:T(8,128)(2,1)} %get-tuple-element.28, bf16[2,1,104,384]{2,3,0,1:T(8,128)(2,1)} %get-tuple-element.29), kind=kLoop, calls=%fused_computation.36 | loop fusion | flops 1437696 | bytes 958464 | tf_op jit(solution)/shard_map/concatenate | solution.py:106
  90.2 1.0 copy.127
  91.2 1.1 pad_maximum_fusion.8
  92.3 1.0 copy.129
  93.4 1.6 %fusion.39 = f32[208,192]{0,1:T(8,128)S(1)} fusion(bf16[208,1152]{1,0:T(8,128)(2,1)} %bitcast.162, bf16[1152,192]{0,1:T(8,128)(2,1)} %bitcast.163), kind=kOutput, calls=%fused_computation.102 | convolution fusion | flops 92012544 | bytes 1081344 | tf_op jit(solution)/shard_map/dot_general | solution.py:107
  99.9 4.9 %all-reduce.2 = (f32[2,16]{1,0:T(2,128)S(1)}, f32[2,16]{1,0:T(2,128)S(1)}) all-reduce(f32[2,16]{1,0:T(2,128)S(1)} %copy.133, f32[2,16]{1,0:T(2,128)S(1)} %copy.131), channel_id=1, replica_groups=mesh['video'=2,'block'=4,'band'=2,'chan'=2] {'band'}, use_global_device_ids=true, to_apply=%region_13.14 | all-reduce | flops 64 | bytes 512 | tf_op jit(solution)/shard_map/psum | solution.py:48
  105.4 14.3 %all_gather.11 = bf16[8,1,104,192]{2,3,1,0:T(8,128)(2,1)S(1)} all-gather(bf16[2,1,104,192]{2,3,1,0:T(8,128)(2,1)S(1)} %multiply_convert_fusion.1), channel_id=1, replica_groups=mesh['video'=2,'block'=4,'band'=2,'chan'=2] {'block'}, dimensions={0}, use_global_device_ids=true | all-gather | bytes 399360 | tf_op jit(solution)/shard_map/all_gather | solution.py:157
  119.8 0.6 gather_fusion.2
  120.4 0.8 fusion.17
  (115 shorter events, 10.7 us)
Async XLA Ops:
  0.0 29.9 %copy-start = (bf16[3,3,3,16,384]{4,3,2,1,0:T(8,128)(2,1)S(1)}, bf16[3,3,3,16,384]{4,3,2,1,0:T(8,128)(2,1)}, u32[]{:S(2)}) copy-start(bf16[3,3,3,16,384]{4,3,2,1,0:T(8,128)(2,1)} %param.10) | copy-start | bytes 995332
  19.5 15.0 %collective-permute-start.1 = (bf16[6,1,1664]{2,0,1:T(8,128)(2,1)S(1)}, bf16[6,1,1664]{2,0,1:T(8,128)(2,1)S(1)}, u32[]{:S(2)}, u32[]{:S(2)}) collective-permute-start(bf16[6,1,1664]{2,0,1:T(8,128)(2,1)S(1)} %fusion.21), channel_id=1, source_target_pairs={{2,0},{3,1},{6,4},{7,5},{10,8},{11,9},{14,12},{15,13},{18,16},{19,... | collective-permute-start | bytes 59912 | tf_op jit(solution)/shard_map/ppermute | solution.py:22
  20.8 13.9 %collective-permute-start = (bf16[6,1,1664]{2,0,1:T(8,128)(2,1)S(1)}, bf16[6,1,1664]{2,0,1:T(8,128)(2,1)S(1)}, u32[]{:S(2)}, u32[]{:S(2)}) collective-permute-start(bf16[6,1,1664]{2,0,1:T(8,128)(2,1)S(1)} %fusion.21), channel_id=1, source_target_pairs={{0,2},{1,3},{4,6},{5,7},{8,10},{9,11},{12,14},{13,15},{16,18},{17,... | collective-permute-start | bytes 59912 | tf_op jit(solution)/shard_map/ppermute | solution.py:20
  26.4 6.8 %copy-start.25 = (f32[384]{0:T(512)S(1)}, f32[384]{0:T(512)}, u32[]{:S(2)}) copy-start(f32[384]{0:T(512)} %param.12) | copy-start | bytes 4612
  26.4 7.5 %copy-start.26 = (f32[384]{0:T(512)S(1)}, f32[384]{0:T(512)}, u32[]{:S(2)}) copy-start(f32[384]{0:T(512)} %param.11) | copy-start | bytes 4612
  35.1 7.5 %copy-start.16 = (bf16[4,1,104,16]{3,2,0,1:T(8,128)(2,1)S(1)}, bf16[4,1,104,16]{3,2,0,1:T(8,128)(2,1)}, u32[]{:S(2)}) copy-start(bf16[4,1,104,16]{3,2,0,1:T(8,128)(2,1)} %get-tuple-element.69) | copy-start | bytes 39940
  35.1 7.5 %copy-start.17 = (bf16[4,1,104,16]{3,2,0,1:T(8,128)(2,1)S(1)}, bf16[4,1,104,16]{3,2,0,1:T(8,128)(2,1)}, u32[]{:S(2)}) copy-start(bf16[4,1,104,16]{3,2,0,1:T(8,128)(2,1)} %get-tuple-element.70) | copy-start | bytes 39940
  35.1 7.5 %copy-start.18 = (bf16[4,1,104,16]{3,2,0,1:T(8,128)(2,1)S(1)}, bf16[4,1,104,16]{3,2,0,1:T(8,128)(2,1)}, u32[]{:S(2)}) copy-start(bf16[4,1,104,16]{3,2,0,1:T(8,128)(2,1)} %get-tuple-element.71) | copy-start | bytes 39940
  46.5 7.9 %copy-start.19 = (f32[192]{0:T(256)S(1)}, f32[192]{0:T(256)}, u32[]{:S(2)}) copy-start(f32[192]{0:T(256)} %dynamic_slice.11) | copy-start | bytes 2308
  46.5 7.9 %copy-start.20 = (f32[192]{0:T(256)S(1)}, f32[192]{0:T(256)}, u32[]{:S(2)}) copy-start(f32[192]{0:T(256)} %dynamic_slice.10) | copy-start | bytes 2308
  46.5 7.9 %copy-start.27 = (pred[4]{0:T(512)(128)(4,1)S(1)}, pred[4]{0:T(512)(128)(4,1)}, u32[]{:S(2)}) copy-start(pred[4]{0:T(512)(128)(4,1)} %add_compare_fusion) | copy-start | bytes 16
  46.5 15.8 %copy-start.14 = (bf16[1,1,3,384,192]{3,4,2,1,0:T(8,128)(2,1)S(1)}, bf16[1,1,3,384,192]{3,4,2,1,0:T(8,128)(2,1)}, u32[]{:S(2)}) copy-start(bf16[1,1,3,384,192]{3,4,2,1,0:T(8,128)(2,1)} %get-tuple-element.22) | copy-start | bytes 1327108
  55.8 18.1 %collective-permute-start.3 = (bf16[4,1,104,192]{2,3,0,1:T(8,128)(2,1)S(1)}, bf16[4,1,104,192]{2,3,0,1:T(8,128)(2,1)S(1)}, u32[]{:S(2)}, u32[]{:S(2)}) collective-permute-start(bf16[4,1,104,192]{2,3,0,1:T(8,128)(2,1)S(1)} %select_bitcast_fusion), channel_id=1, source_target_pairs={{2,0},{3,1},{6,4},{7,5},{10,8},{11,9},{14,12},{15,13},{18,16},{19,... | collective-permute-start | bytes 479240 | tf_op jit(solution)/shard_map/ppermute | solution.py:22
  57.1 16.8 %collective-permute-start.2 = (bf16[4,1,104,192]{2,3,0,1:T(8,128)(2,1)S(1)}, bf16[4,1,104,192]{2,3,0,1:T(8,128)(2,1)S(1)}, u32[]{:S(2)}, u32[]{:S(2)}) collective-permute-start(bf16[4,1,104,192]{2,3,0,1:T(8,128)(2,1)S(1)} %select_bitcast_fusion), channel_id=1, source_target_pairs={{0,2},{1,3},{4,6},{5,7},{8,10},{9,11},{12,14},{13,15},{16,18},{17,... | collective-permute-start | bytes 479240 | tf_op jit(solution)/shard_map/ppermute | solution.py:20
  62.7 1.1 copy-start.13
  64.2 1.1 copy-start.12
  80.9 0.9 copy-start.15
  93.4 1.6 %copy-start.4 = (bf16[24,8,3,384]{3,1,2,0:T(8,128)(2,1)S(1)}, bf16[24,8,3,384]{3,1,2,0:T(8,128)(2,1)}, u32[]{:S(2)}) copy-start(bf16[24,8,3,384]{3,1,2,0:T(8,128)(2,1)} %copy.139) | copy-start | bytes 1327108
  93.4 1.9 %copy-start.5 = (bf16[24,8,3,384]{3,1,2,0:T(8,128)(2,1)S(1)}, bf16[24,8,3,384]{3,1,2,0:T(8,128)(2,1)}, u32[]{:S(2)}) copy-start(bf16[24,8,3,384]{3,1,2,0:T(8,128)(2,1)} %copy.140) | copy-start | bytes 1327108
  94.9 1.0 copy-start.6
  95.3 1.0 copy-start.7
  96.0 1.0 copy-start.8
  96.3 1.1 copy-start.1
  96.4 1.2 copy-start.9
  97.0 1.1 copy-start.2
  97.0 1.2 %copy-start.10 = (bf16[24,8,3,384]{3,1,2,0:T(8,128)(2,1)S(1)}, bf16[24,8,3,384]{3,1,2,0:T(8,128)(2,1)}, u32[]{:S(2)}) copy-start(bf16[24,8,3,384]{3,1,2,0:T(8,128)(2,1)} %copy.145) | copy-start | bytes 1327108
  97.5 1.1 copy-start.3
  97.5 1.2 %copy-start.11 = (bf16[24,8,3,384]{3,1,2,0:T(8,128)(2,1)S(1)}, bf16[24,8,3,384]{3,1,2,0:T(8,128)(2,1)}, u32[]{:S(2)}) copy-start(bf16[24,8,3,384]{3,1,2,0:T(8,128)(2,1)} %copy.146) | copy-start | bytes 1327108
  98.8 6.4 %copy-start.23 = (f32[192]{0:T(256)S(1)}, f32[192]{0:T(256)}, u32[]{:S(2)}) copy-start(f32[192]{0:T(256)} %param.15) | copy-start | bytes 2308
  98.8 6.4 %copy-start.24 = (f32[192]{0:T(256)S(1)}, f32[192]{0:T(256)}, u32[]{:S(2)}) copy-start(f32[192]{0:T(256)} %param.14) | copy-start | bytes 2308
  99.1 21.3 %copy-start.21 = (pred[4]{0:T(512)(128)(4,1)S(1)}, pred[4]{0:T(512)(128)(4,1)}, u32[]{:S(2)}) copy-start(pred[4]{0:T(512)(128)(4,1)} %get-tuple-element.84) | copy-start | bytes 16
  99.1 21.3 %copy-start.22 = (pred[4]{0:T(512)(128)(4,1)S(1)}, pred[4]{0:T(512)(128)(4,1)}, u32[]{:S(2)}) copy-start(pred[4]{0:T(512)(128)(4,1)} %get-tuple-element.85) | copy-start | bytes 16
where the time goes:
time: 122 us; the launch traced here: 121 us
  local copies, waits for them, and re-layouts  44.2 us (36%)
  blocking collectives  42.1 us (35%)
  other arithmetic  16.3 us (13%)
  starting transfers between devices  11.7 us (10%)
  matrix products  6.32 us (5%)
    all_gather x1, blocking collectives, shards(): all_slots = lax.all_gather(latents, 'block', axis=0, tiled=True)  15.1 us
    all_gather x1, blocking collectives, shards(): piece = lax.all_gather(even_norm, 'block', axis=0, tiled=True)  14.3 us
    unnamed x67, local copies, waits for them, and re-layouts  11 us
    psum x2, blocking collectives, group_silu(): lax.psum((jnp.sum(grouped, axis=(1, 3)), jnp.sum(grouped * grouped, axis=...  9.83 us
    ppermute x2, starting transfers between devices, with_halo(): lax.ppermute(tail, axis, [(i, (i + 1) % count) for i in range(ends)])  9.11 us
    slice x10, local copies, waits for them, and re-layouts, latent_conv(): latent_grid[step_t:step_t + out_frames, step_y:step_y + band_rows, step_x...  8.19 us
    concatenate x9, other arithmetic, weighted_taps(): stacked = jnp.concatenate(patches, axis=-1).reshape(-1, 3 * in_width)  7.39 us
    slice x10, local copies, waits for them, and re-layouts, weighted_taps(): kernel[step_t, step_y].reshape(3 * in_width, out_width)  6.99 us
  transfers between devices with their start and end apart: 4, of which 0 were waited for; matrix products, arithmetic and copies ran while one was open for 17% of the time, Pallas kernels for 0%

commit v1 on v0

--- a/solution.py
+++ b/solution.py
@@ -154,7 +154,16 @@
     slot_frames = my_start + slot_places
     slot_alive = slot_places < live_count
     initial = jnp.zeros((frames, band_rows, columns, half_width), jnp.bfloat16)
-    piece = lax.all_gather(even_norm, "block", axis=0, tiled=True)
+    q_n = jax.lax.axis_size("block")
+    made = [(dev, (dev + 1) % q_n) for dev in range(q_n)]
+    cards = [(dev, (dev - 1) % q_n) for dev in range(q_n)]
+    long_array, mid_arr = ([even_norm], [even_norm])
+    for _ in range(q_n // 2):
+        long_array.append(jax.lax.ppermute(long_array[-1], "block", made))
+    for _ in range((q_n - 1) // 2):
+        mid_arr.append(jax.lax.ppermute(mid_arr[-1], "block", cards))
+    e_now = jnp.concatenate([*long_array[::-1], *mid_arr[1:]], 0)
+    piece = jnp.roll(e_now, (jax.lax.axis_index("block") - q_n // 2) * even_norm.shape[0], 0)
     valid = (slot_frames >= 0) & (slot_frames < piece.shape[0]) & slot_alive
     took = jnp.take(piece, jnp.clip(slot_frames, 0, piece.shape[0] - 1), axis=0)
     return jnp.where(valid[:, None, None, None], took, initial)

time: 122 us -> 113 us (0.926)
  blocking collectives: 42.1 us -> 28 us
  waiting for transfers between devices: 0.01 us -> 8.8 us
  local copies, waits for them, and re-layouts: 44.2 us -> 36.2 us
  starting transfers between devices: 11.7 us -> 17.1 us
  matrix products: 6.32 us -> 4.74 us
    all_gather x1 -> x0, blocking collectives: 14.3 us -> none  [shards(): piece = lax.all_gather(even_norm, 'block', axis=0, tiled=True)]
    ppermute x0 -> x3, waiting for transfers between devices: none -> 8.12 us  [the longest x2 8.12 us: shards(): long_array.append(jax.lax.ppermute(long_array[-1], 'block', made))]
    slice x10, local copies, waits for them, and re-layouts: 8.19 us -> 1.87 us  [latent_conv(): latent_grid[step_t:step_t + out_frames, step_y:step_y + band_rows, step_x...]
    ppermute x0 -> x3, starting transfers between devices: none -> 4.13 us  [the longest x1 2.17 us: shards(): mid_arr.append(jax.lax.ppermute(mid_arr[-1], 'block', cards))]
    dot_general x1, matrix products: 2.2 us -> 0.63 us  [latent_conv(): jnp.dot(stacked, kernel.reshape(27 * lat_width, out_width), preferred_ele...]
    concatenate x1, local copies, waits for them, and re-layouts: 3.95 us -> 2.54 us  [latent_conv(): stacked = jnp.concatenate(patches, axis=-1).reshape(-1, 27 * lat_width)]
    concatenate x0 -> x1, local copies, waits for them, and re-layouts: none -> 1.4 us  [shards(): jnp.roll(e_now, (jax.lax.axis_index('block') - q_n // 2) * even_norm.shap...]
    ppermute x2, starting transfers between devices: 9.11 us -> 10.4 us  [with_halo(): lax.ppermute(tail, axis, [(i, (i + 1) % count) for i in range(ends)])]
  transfers between devices with their start and end apart: 4 -> 7, of which waited for: 0 -> 3; matrix products, arithmetic and copies ran while one was open for 17% -> 16% of each run, Pallas kernels for 0% -> 0%
where the time goes in v1:
time: 113 us; the launch traced here: 112 us
  local copies, waits for them, and re-layouts  36.2 us (32%)
  blocking collectives  28 us (25%)
  starting transfers between devices  17.1 us (15%)
  other arithmetic  16.4 us (15%)
  waiting for transfers between devices  8.8 us (8%)
  matrix products  4.74 us (4%)
    all_gather x1, blocking collectives, shards(): all_slots = lax.all_gather(latents, 'block', axis=0, tiled=True)  15.1 us
    ppermute x2, starting transfers between devices, with_halo(): lax.ppermute(tail, axis, [(i, (i + 1) % count) for i in range(ends)])  10.4 us
    psum x2, blocking collectives, group_silu(): lax.psum((jnp.sum(grouped, axis=(1, 3)), jnp.sum(grouped * grouped, axis=...  10.1 us
    unnamed x45, local copies, waits for them, and re-layouts  9.98 us
    ppermute x2, waiting for transfers between devices, shards(): long_array.append(jax.lax.ppermute(long_array[-1], 'block', made))  8.12 us
    slice x10, local copies, waits for them, and re-layouts, weighted_taps(): kernel[step_t, step_y].reshape(3 * in_width, out_width)  7.9 us
    concatenate x9, other arithmetic, weighted_taps(): stacked = jnp.concatenate(patches, axis=-1).reshape(-1, 3 * in_width)  7.29 us
    concatenate x9, local copies, waits for them, and re-layouts, weighted_taps(): stacked = jnp.concatenate(patches, axis=-1).reshape(-1, 3 * in_width)  5.64 us
  transfers between devices with their start and end apart: 7, of which 3 were waited for; matrix products, arithmetic and copies ran while one was open for 16% of the time, Pallas kernels for 0%

profile of v1, /device:TPU:0, one launch (start us, length us, event | category | flops | bytes accessed | tf_op | source)
XLA Modules:
  0.0 112.0 jit_solution(9276626293088189438)
XLA Ops:
  0.0 0.9 reduce-window.8
  0.9 1.3 %fusion.21 = (s32[]{:T(128)}, s32[]{:T(128)}, s32[4]{0:T(128)S(1)}) fusion(s32[4]{0:T(128)} %param.9, s32[]{:T(128)S(6)} %axis_index.27, s32[4,1]{0,1:T(1,128)S(1)} %reduce-window.8), kind=kLoop, calls=%fused_computation.76 | loop fusion | flops 26 | bytes 60 | tf_op jit(solution)/shard_map/reduce_sum | solution.py:31
  2.3 0.6 gather_fusion
  3.0 0.7 copy.119
  3.7 15.1 %all_gather.6 = bf16[16,1,1664]{2,1,0:T(2,128)(2,1)S(1)} all-gather(bf16[4,1,1664]{2,1,0:T(2,128)(2,1)S(1)} %copy.119), channel_id=1, replica_groups=mesh['video'=2,'block'=4,'band'=2,'chan'=2] {'block'}, dimensions={0}, use_global_device_ids=true | all-gather | bytes 66560 | tf_op jit(solution)/shard_map/all_gather | solution.py:133
  18.8 0.6 gather_fusion.1
  19.5 1.3 %collective-permute-start.1 = (bf16[6,1,1664]{2,0,1:T(8,128)(2,1)S(1)}, bf16[6,1,1664]{2,0,1:T(8,128)(2,1)S(1)}, u32[]{:S(2)}, u32[]{:S(2)}) collective-permute-start(bf16[6,1,1664]{2,0,1:T(8,128)(2,1)S(1)} %fusion.19), channel_id=1, source_target_pairs={{2,0},{3,1},{6,4},{7,5},{10,8},{11,9},{14,12},{15,13},{18,16},{19,... | collective-permute-start | bytes 59912 | tf_op jit(solution)/shard_map/ppermute | solution.py:22
  20.8 4.5 %collective-permute-start = (bf16[6,1,1664]{2,0,1:T(8,128)(2,1)S(1)}, bf16[6,1,1664]{2,0,1:T(8,128)(2,1)S(1)}, u32[]{:S(2)}, u32[]{:S(2)}) collective-permute-start(bf16[6,1,1664]{2,0,1:T(8,128)(2,1)S(1)} %fusion.19), channel_id=1, source_target_pairs={{0,2},{1,3},{4,6},{5,7},{8,10},{9,11},{12,14},{13,15},{16,18},{17,... | collective-permute-start | bytes 59912 | tf_op jit(solution)/shard_map/ppermute | solution.py:20
  26.2 0.7 collective-permute-done
  27.2 1.0 fusion.33
  29.1 2.5 %concatenate.50 = bf16[4,1,104,432]{3,2,0,1:T(8,128)(2,1)S(1)} concatenate(bf16[4,1,104,16]{3,2,0,1:T(8,128)(2,1)} %get-tuple-element.68, bf16[4,1,104,16]{3,2,0,1:T(8,128)(2,1)S(1)} %slice.227, bf16[4,1,104,16]{3,2,0,1:T(8,128)(2,1)} %get-tuple-element.67, bf16[4,1,104,16]{3,2,0,1:T(8,128)(2,1)} %get-tuple-element.66, bf16[4,1,104,16]{3,2,0,1:T(8,128)(2,1)S(1)} %get-tuple-element.71, ...), dimensions={3} | concatenate | bytes 718848 | tf_op jit(solution)/shard_map/concatenate | solution.py:81
  31.7 0.6 fusion.28
  32.7 5.2 %all-reduce.3 = (f32[4,16]{1,0:T(4,128)S(1)}, f32[4,16]{1,0:T(4,128)S(1)}) all-reduce(f32[4,16]{1,0:T(4,128)S(1)} %reduce_sum.88, f32[4,16]{1,0:T(4,128)S(1)} %reduce_sum.85), channel_id=1, replica_groups=mesh['video'=2,'block'=4,'band'=2,'chan'=2] {'band'}, use_global_device_ids=true, to_apply=%region_9.10 | all-reduce | flops 128 | bytes 1024 | tf_op jit(solution)/shard_map/psum | solution.py:48
  38.2 1.0 select_bitcast_fusion
  39.3 1.3 %collective-permute-start.3 = (bf16[4,1,104,192]{2,3,0,1:T(8,128)(2,1)}, bf16[4,1,104,192]{2,3,0,1:T(8,128)(2,1)}, u32[]{:S(2)}, u32[]{:S(2)}) collective-permute-start(bf16[4,1,104,192]{2,3,0,1:T(8,128)(2,1)} %select_bitcast_fusion), channel_id=1, source_target_pairs={{2,0},{3,1},{6,4},{7,5},{10,8},{11,9},{14,12},{15,13},{18,16},{19,... | collective-permute-start | bytes 479240 | tf_op jit(solution)/shard_map/ppermute | solution.py:22
  40.6 5.9 %collective-permute-start.2 = (bf16[4,1,104,192]{2,3,0,1:T(8,128)(2,1)}, bf16[4,1,104,192]{2,3,0,1:T(8,128)(2,1)}, u32[]{:S(2)}, u32[]{:S(2)}) collective-permute-start(bf16[4,1,104,192]{2,3,0,1:T(8,128)(2,1)} %select_bitcast_fusion), channel_id=1, source_target_pairs={{0,2},{1,3},{4,6},{5,7},{8,10},{9,11},{12,14},{13,15},{16,18},{17,... | collective-permute-start | bytes 479240 | tf_op jit(solution)/shard_map/ppermute | solution.py:20
  46.4 3.4 %fusion.30 = (bf16[1,1,3,384,192]{3,4,2,1,0:T(8,128)(2,1)S(1)}, bf16[1,1,3,384,192]{3,4,2,1,0:T(8,128)(2,1)S(1)}, bf16[1,1,3,384,192]{3,4,2,1,0:T(8,128)(2,1)S(1...) fusion(bf16[3,3,3,384,192]{3,4,2,1,0:T(8,128)(2,1)} %param.13), kind=kLoop, calls=%fused_computation.94 | loop fusion | bytes 7962624 | tf_op jit(solution)/shard_map/slice | solution.py:109
  49.9 1.4 %copy.122 = bf16[1,1,3,384,192]{3,2,4,1,0:T(4,128)(2,1)S(1)} copy(bf16[1,1,3,384,192]{3,4,2,1,0:T(8,128)(2,1)} %get-tuple-element.22) | data formatting | bytes 884736 | tf_op jit(solution)/shard_map/slice | solution.py:109
  51.3 0.8 copy.148
  52.4 0.4 copy.124
  52.8 0.8 copy.149
  53.6 0.4 copy.126
  54.0 0.8 copy.150
  54.9 0.4 copy.128
  55.2 0.8 copy.151
  56.1 0.4 copy.130
  56.5 0.8 copy.152
  57.3 0.4 copy.132
  57.7 0.8 copy.153
  58.5 0.4 copy.134
  58.9 0.8 copy.154
  59.7 0.4 copy.136
  60.1 0.8 copy.155
  60.9 0.4 copy.138
  61.3 0.8 copy.156
  62.1 0.6 fusion.25
  62.7 1.4 %fusion.12 = bf16[4,3,106,192]{2,3,0,1:T(8,128)(2,1)S(1)} fusion(bf16[4,1,104,192]{2,3,0,1:T(8,128)(2,1)} %collective-permute-done.3, bf16[4,1,104,192]{2,3,0,1:T(8,128)(2,1)} %select_bitcast_fusion, bf16[4,1,104,192]{2,3,0,1:T(8,128)(2,1)} %collective-permute-done.2), kind=kLoop, calls=%fused_computation.28 | loop fusion | flops 2930688 | bytes 967680 | tf_op jit(solution)/shard_map/concatenate | solution.py:18
  64.1 2.8 %all_gather.7 = bf16[4,3,106,384]{2,3,0,1:T(8,128)(2,1)S(1)} all-gather(bf16[4,3,106,192]{2,3,0,1:T(8,128)(2,1)S(1)} %fusion.12), channel_id=1, replica_groups=mesh['video'=2,'block'=4,'band'=2,'chan'=2] {'chan'}, dimensions={3}, use_global_device_ids=true | all-gather | bytes 1465344 | tf_op jit(solution)/shard_map/all_gather | solution.py:117
  67.0 0.3 fusion.32
  67.3 2.2 %fusion.31 = (bf16[2,1,104,384]{2,3,0,1:T(8,128)(2,1)S(1)}, bf16[2,1,104,384]{2,3,0,1:T(8,128)(2,1)}, bf16[2,1,104,384]{2,3,0,1:T(8,128)(2,1)}, bf16[2,1,104,384...) fusion(bf16[4,3,106,384]{2,3,0,1:T(8,128)(2,1)S(1)} %all_gather.7), kind=kLoop, calls=%fused_computation.95 | loop fusion | bytes 6070272 | tf_op jit(solution)/shard_map/slice | solution.py:98
  69.6 1.0 copy.121
  71.5 1.0 pad_maximum_fusion.3
  72.8 1.0 pad_maximum_fusion.4
  74.1 1.2 %pad_maximum_fusion.5 = bf16[2,1,104,1152]{2,3,0,1:T(8,128)(2,1)S(1)} fusion(bf16[2,1,104,384]{2,3,0,1:T(8,128)(2,1)} %get-tuple-element.33, bf16[2,1,104,384]{2,3,0,1:T(8,128)(2,1)} %get-tuple-element.34, bf16[2,1,104,384]{2,3,0,1:T(8,128)(2,1)} %get-tuple-element.35), kind=kLoop, calls=%fused_computation.34 | loop fusion | flops 1437696 | bytes 958464 | tf_op jit(solution)/shard_map/concatenate | solution.py:106
  75.7 1.2 %pad_maximum_fusion.6 = bf16[2,1,104,1152]{2,3,0,1:T(8,128)(2,1)S(1)} fusion(bf16[2,1,104,384]{2,3,0,1:T(8,128)(2,1)} %get-tuple-element.30, bf16[2,1,104,384]{2,3,0,1:T(8,128)(2,1)} %get-tuple-element.31, bf16[2,1,104,384]{2,3,0,1:T(8,128)(2,1)} %get-tuple-element.32), kind=kLoop, calls=%fused_computation.35 | loop fusion | flops 1437696 | bytes 958464 | tf_op jit(solution)/shard_map/concatenate | solution.py:106
  76.9 1.1 copy.133
  78.0 1.2 %pad_maximum_fusion.7 = bf16[2,1,104,1152]{2,3,0,1:T(8,128)(2,1)S(1)} fusion(bf16[2,1,104,384]{2,3,0,1:T(8,128)(2,1)} %get-tuple-element.27, bf16[2,1,104,384]{2,3,0,1:T(8,128)(2,1)} %get-tuple-element.28, bf16[2,1,104,384]{2,3,0,1:T(8,128)(2,1)} %get-tuple-element.29), kind=kLoop, calls=%fused_computation.36 | loop fusion | flops 1437696 | bytes 958464 | tf_op jit(solution)/shard_map/concatenate | solution.py:106
  79.2 1.1 copy.135
  80.3 1.1 %pad_maximum_fusion.8 = bf16[2,1,104,1152]{2,3,0,1:T(8,128)(2,1)S(1)} fusion(bf16[2,1,104,384]{2,3,0,1:T(8,128)(2,1)} %get-tuple-element.25, bf16[2,1,104,384]{2,3,0,1:T(8,128)(2,1)} %get-tuple-element.26, bf16[2,1,104,384]{2,3,0,1:T(8,128)(2,1)S(1)} %get-tuple-element.24), kind=kLoop, calls=%fused_computation.37 | loop fusion | flops 1437696 | bytes 958464 | tf_op jit(solution)/shard_map/concatenate | solution.py:106
  81.4 1.0 copy.137
  82.5 1.6 %fusion.37 = f32[208,192]{0,1:T(8,128)S(1)} fusion(bf16[208,1152]{1,0:T(8,128)(2,1)} %bitcast.164, bf16[1152,192]{0,1:T(8,128)(2,1)} %bitcast.165), kind=kOutput, calls=%fused_computation.101 | convolution fusion | flops 92012544 | bytes 1081344 | tf_op jit(solution)/shard_map/dot_general | solution.py:107
  84.0 0.3 convolution_add_fusion.7
  84.7 0.3 copy-done.6
  85.8 0.3 copy-done.8
  89.0 4.9 %all-reduce.2 = (f32[2,16]{1,0:T(2,128)S(1)}, f32[2,16]{1,0:T(2,128)S(1)}) all-reduce(f32[2,16]{1,0:T(2,128)S(1)} %copy.141, f32[2,16]{1,0:T(2,128)S(1)} %copy.139), channel_id=1, replica_groups=mesh['video'=2,'block'=4,'band'=2,'chan'=2] {'band'}, use_global_device_ids=true, to_apply=%region_13.14 | all-reduce | flops 64 | bytes 512 | tf_op jit(solution)/shard_map/psum | solution.py:48
  94.5 1.0 fusion.18
  95.5 1.7 %collective-permute-start.4 = (bf16[2,1,104,192]{2,0,3,1:T(2,128)(2,1)S(1)}, bf16[2,1,104,192]{2,0,3,1:T(2,128)(2,1)S(1)}, u32[]{:S(2)}, u32[]{:S(2)}) collective-permute-start(bf16[2,1,104,192]{2,0,3,1:T(2,128)(2,1)S(1)} %fusion.18), channel_id=1, source_target_pairs={{0,4},{4,8},{8,12},{12,0},{1,5},{5,9},{9,13},{13,1},{2,6},{6,10},{... | collective-permute-start | bytes 239624 | tf_op jit(solution)/shard_map/ppermute | solution.py:162
  97.3 2.2 %collective-permute-start.6 = (bf16[2,1,104,192]{2,0,3,1:T(2,128)(2,1)S(1)}, bf16[2,1,104,192]{2,0,3,1:T(2,128)(2,1)S(1)}, u32[]{:S(2)}, u32[]{:S(2)}) collective-permute-start(bf16[2,1,104,192]{2,0,3,1:T(2,128)(2,1)S(1)} %fusion.18), channel_id=1, source_target_pairs={{0,12},{4,0},{8,4},{12,8},{1,13},{5,1},{9,5},{13,9},{2,14},{6,2},{... | collective-permute-start | bytes 239624 | tf_op jit(solution)/shard_map/ppermute | solution.py:164
  99.4 3.2 %collective-permute-done.4 = bf16[2,1,104,192]{2,0,3,1:T(2,128)(2,1)S(1)} collective-permute-done((bf16[2,1,104,192]{2,0,3,1:T(2,128)(2,1)S(1)}, bf16[2,1,104,192]{2,0,3,1:T(2,128)(2,1)S(1)}, u32[]{:S(2)}, u32[]{:S(2)}) %collective-permute-start.4) | collective-permute-done | bytes 79904 | tf_op jit(solution)/shard_map/ppermute | solution.py:162
  102.9 1.2 %compare_and_fusion.1 = (pred[4]{0:T(512)(128)(4,1)S(1)}, pred[4]{0:T(512)(128)(4,1)S(1)}) fusion(s32[]{:T(128)} %get-tuple-element.10, s32[]{:T(128)} %get-tuple-element.9), kind=kLoop, calls=%fused_computation.69 | loop fusion | flops 52 | bytes 16 | tf_op jit(solution)/shard_map/jit(_take)/and | solution.py:168
  104.1 5.0 %collective-permute-done.5 = bf16[2,1,104,192]{2,0,3,1:T(2,128)(2,1)S(1)} collective-permute-done((bf16[2,1,104,192]{2,0,3,1:T(2,128)(2,1)S(1)}, bf16[2,1,104,192]{2,0,3,1:T(2,128)(2,1)S(1)}, u32[]{:S(2)}, u32[]{:S(2)}) %collective-permute-start.5) | collective-permute-done | bytes 79904 | tf_op jit(solution)/shard_map/ppermute | solution.py:162
  109.0 1.4 %concatenate.61 = bf16[16,1,104,192]{2,0,3,1:T(8,128)(2,1)S(1)} concatenate(bf16[2,1,104,192]{2,0,3,1:T(2,128)(2,1)S(1)} %collective-permute-done.5, bf16[2,1,104,192]{2,0,3,1:T(2,128)(2,1)S(1)} %collective-permute-done.4, bf16[2,1,104,192]{2,0,3,1:T(2,128)(2,1)S(1)} %fusion.18, bf16[2,1,104,192]{2,0,3,1:T(2,128)(2,1)S(1)} %collective-permute-done.6, ...), dimensions={0} | concatenate | bytes 1277952 | tf_op jit(solution)/shard_map/jit(_roll_dynamic)/concatenate | solution.py:166
  110.6 0.6 gather_fusion.2
  111.2 0.8 fusion.17
  (103 shorter events, 9.9 us)
Async XLA Ops:
  0.0 25.7 %copy-start = (bf16[3,3,3,16,384]{4,3,2,1,0:T(8,128)(2,1)S(1)}, bf16[3,3,3,16,384]{4,3,2,1,0:T(8,128)(2,1)}, u32[]{:S(2)}) copy-start(bf16[3,3,3,16,384]{4,3,2,1,0:T(8,128)(2,1)} %param.10) | copy-start | bytes 995332
  2.9 22.9 %copy-start.15 = (f32[384]{0:T(512)S(1)}, f32[384]{0:T(512)}, u32[]{:S(2)}) copy-start(f32[384]{0:T(512)} %param.12) | copy-start | bytes 4612
  2.9 23.0 %copy-start.16 = (f32[384]{0:T(512)S(1)}, f32[384]{0:T(512)}, u32[]{:S(2)}) copy-start(f32[384]{0:T(512)} %param.11) | copy-start | bytes 4612
  19.5 6.5 %collective-permute-start.1 = (bf16[6,1,1664]{2,0,1:T(8,128)(2,1)S(1)}, bf16[6,1,1664]{2,0,1:T(8,128)(2,1)S(1)}, u32[]{:S(2)}, u32[]{:S(2)}) collective-permute-start(bf16[6,1,1664]{2,0,1:T(8,128)(2,1)S(1)} %fusion.19), channel_id=1, source_target_pairs={{2,0},{3,1},{6,4},{7,5},{10,8},{11,9},{14,12},{15,13},{18,16},{19,... | collective-permute-start | bytes 59912 | tf_op jit(solution)/shard_map/ppermute | solution.py:22
  20.8 6.1 %collective-permute-start = (bf16[6,1,1664]{2,0,1:T(8,128)(2,1)S(1)}, bf16[6,1,1664]{2,0,1:T(8,128)(2,1)S(1)}, u32[]{:S(2)}, u32[]{:S(2)}) collective-permute-start(bf16[6,1,1664]{2,0,1:T(8,128)(2,1)S(1)} %fusion.19), channel_id=1, source_target_pairs={{0,2},{1,3},{4,6},{5,7},{8,10},{9,11},{12,14},{13,15},{16,18},{17,... | collective-permute-start | bytes 59912 | tf_op jit(solution)/shard_map/ppermute | solution.py:20
  39.3 23.4 %collective-permute-start.3 = (bf16[4,1,104,192]{2,3,0,1:T(8,128)(2,1)}, bf16[4,1,104,192]{2,3,0,1:T(8,128)(2,1)}, u32[]{:S(2)}, u32[]{:S(2)}) collective-permute-start(bf16[4,1,104,192]{2,3,0,1:T(8,128)(2,1)} %select_bitcast_fusion), channel_id=1, source_target_pairs={{2,0},{3,1},{6,4},{7,5},{10,8},{11,9},{14,12},{15,13},{18,16},{19,... | collective-permute-start | bytes 479240 | tf_op jit(solution)/shard_map/ppermute | solution.py:22
  40.6 22.1 %collective-permute-start.2 = (bf16[4,1,104,192]{2,3,0,1:T(8,128)(2,1)}, bf16[4,1,104,192]{2,3,0,1:T(8,128)(2,1)}, u32[]{:S(2)}, u32[]{:S(2)}) collective-permute-start(bf16[4,1,104,192]{2,3,0,1:T(8,128)(2,1)} %select_bitcast_fusion), channel_id=1, source_target_pairs={{0,2},{1,3},{4,6},{5,7},{8,10},{9,11},{12,14},{13,15},{16,18},{17,... | collective-permute-start | bytes 479240 | tf_op jit(solution)/shard_map/ppermute | solution.py:20
  51.3 1.1 %copy-start.12 = (bf16[1,1,3,384,192]{3,4,2,1,0:T(8,128)(2,1)S(1)}, bf16[1,1,3,384,192]{3,4,2,1,0:T(8,128)(2,1)}, u32[]{:S(2)}) copy-start(bf16[1,1,3,384,192]{3,4,2,1,0:T(8,128)(2,1)} %get-tuple-element.21) | copy-start | bytes 1327108
  82.4 1.6 %copy-start.4 = (bf16[24,8,3,384]{3,1,2,0:T(8,128)(2,1)S(1)}, bf16[24,8,3,384]{3,1,2,0:T(8,128)(2,1)}, u32[]{:S(2)}) copy-start(bf16[24,8,3,384]{3,1,2,0:T(8,128)(2,1)} %copy.149) | copy-start | bytes 1327108
  82.5 1.9 %copy-start.5 = (bf16[24,8,3,384]{3,1,2,0:T(8,128)(2,1)S(1)}, bf16[24,8,3,384]{3,1,2,0:T(8,128)(2,1)}, u32[]{:S(2)}) copy-start(bf16[24,8,3,384]{3,1,2,0:T(8,128)(2,1)} %copy.150) | copy-start | bytes 1327108
  84.0 1.0 copy-start.6
  84.4 1.0 copy-start.7
  85.0 1.0 copy-start.8
  85.4 1.1 copy-start.1
  85.4 1.2 %copy-start.9 = (bf16[24,8,3,384]{3,1,2,0:T(8,128)(2,1)S(1)}, bf16[24,8,3,384]{3,1,2,0:T(8,128)(2,1)}, u32[]{:S(2)}) copy-start(bf16[24,8,3,384]{3,1,2,0:T(8,128)(2,1)} %copy.154) | copy-start | bytes 1327108
  86.1 1.1 copy-start.2
  86.1 1.2 %copy-start.10 = (bf16[24,8,3,384]{3,1,2,0:T(8,128)(2,1)S(1)}, bf16[24,8,3,384]{3,1,2,0:T(8,128)(2,1)}, u32[]{:S(2)}) copy-start(bf16[24,8,3,384]{3,1,2,0:T(8,128)(2,1)} %copy.155) | copy-start | bytes 1327108
  86.6 1.1 copy-start.3
  86.6 1.2 %copy-start.11 = (bf16[24,8,3,384]{3,1,2,0:T(8,128)(2,1)S(1)}, bf16[24,8,3,384]{3,1,2,0:T(8,128)(2,1)}, u32[]{:S(2)}) copy-start(bf16[24,8,3,384]{3,1,2,0:T(8,128)(2,1)} %copy.156) | copy-start | bytes 1327108
  87.8 6.6 %copy-start.13 = (f32[192]{0:T(256)S(1)}, f32[192]{0:T(256)}, u32[]{:S(2)}) copy-start(f32[192]{0:T(256)} %param.15) | copy-start | bytes 2308
  87.8 6.6 %copy-start.14 = (f32[192]{0:T(256)S(1)}, f32[192]{0:T(256)}, u32[]{:S(2)}) copy-start(f32[192]{0:T(256)} %param.14) | copy-start | bytes 2308
  95.5 7.0 %collective-permute-start.4 = (bf16[2,1,104,192]{2,0,3,1:T(2,128)(2,1)S(1)}, bf16[2,1,104,192]{2,0,3,1:T(2,128)(2,1)S(1)}, u32[]{:S(2)}, u32[]{:S(2)}) collective-permute-start(bf16[2,1,104,192]{2,0,3,1:T(2,128)(2,1)S(1)} %fusion.18), channel_id=1, source_target_pairs={{0,4},{4,8},{8,12},{12,0},{1,5},{5,9},{9,13},{13,1},{2,6},{6,10},{... | collective-permute-start | bytes 239624 | tf_op jit(solution)/shard_map/ppermute | solution.py:162
  97.3 6.8 %collective-permute-start.6 = (bf16[2,1,104,192]{2,0,3,1:T(2,128)(2,1)S(1)}, bf16[2,1,104,192]{2,0,3,1:T(2,128)(2,1)S(1)}, u32[]{:S(2)}, u32[]{:S(2)}) collective-permute-start(bf16[2,1,104,192]{2,0,3,1:T(2,128)(2,1)S(1)} %fusion.18), channel_id=1, source_target_pairs={{0,12},{4,0},{8,4},{12,8},{1,13},{5,1},{9,5},{13,9},{2,14},{6,2},{... | collective-permute-start | bytes 239624 | tf_op jit(solution)/shard_map/ppermute | solution.py:164
  102.6 6.4 %collective-permute-start.5 = (bf16[2,1,104,192]{2,0,3,1:T(2,128)(2,1)S(1)}, bf16[2,1,104,192]{2,0,3,1:T(2,128)(2,1)S(1)}, u32[]{:S(2)}, u32[]{:S(2)}) collective-permute-start(bf16[2,1,104,192]{2,0,3,1:T(2,128)(2,1)S(1)} %collective-permute-done.4), channel_id=1, source_target_pairs={{0,4},{4,8},{8,12},{12,0},{1,5},{5,9},{9,13},{13,1},{2,6},{6,10},{... | collective-permute-start | bytes 239624 | tf_op jit(solution)/shard_map/ppermute | solution.py:162
